TPU v7x, 32 devices: a whole 2x2x4 slice. The times are simulated.
32 devices in a mesh: dp: 16 (over z, x, core), tensor: 2 (over y).
Axes of the slice: x: 2, y: 2, z: 4, core: 2. Of those that a mesh axis runs over, the one named last changes fastest.
Arguments:
- inputs: bfloat16 [16384, 1024], P(('dp', 'tensor')), may hold values from -6 to 6
- seg_ids: int32 [32, 512], P('dp'), may hold values from 0 to 15, never falling along the last dimension, each value on 1 to 384 neighbouring positions
- qkv_weight: float32 [2, 3, 1024, 1024], P(None, None, 'dp', 'tensor'), may hold values from -0.1875 to 0.1875
- out_weight: float32 [2, 1024, 1024], P(None, 'tensor', 'dp'), may hold values from -1.5 to 1.5
- up_weight: float32 [2, 1024, 4096], P(None, 'dp', 'tensor'), may hold values from -0.1875 to 0.1875
- down_weight: float32 [2, 4096, 1024], P(None, 'tensor', 'dp'), may hold values from -0.09375 to 0.09375
- norm_gains: float32 [2, 2, 1024], P(None, None, ('dp', 'tensor')), may hold values from 0.5 to 1.5
- row_biases: float32 [2, 6, 1024], P(None, None, ('dp', 'tensor')), may hold values from -2.5 to 2.5
- ff_bias: float32 [2, 4096], P(None, ('dp', 'tensor')), may hold values from -2.5 to 2.5
- cotangent: float32 [16384, 1024], P(('dp', 'tensor')), may hold values from -6 to 6
Outputs:
- outputs: bfloat16 [16384, 1024], P(('dp', 'tensor'))
- input_grad: float32 [16384, 1024], P(('dp', 'tensor'))
- qkv_grad: float32 [2, 3, 1024, 1024], P(None, None, 'dp', 'tensor')
- out_grad: float32 [2, 1024, 1024], P(None, 'tensor', 'dp')
- up_grad: float32 [2, 1024, 4096], P(None, 'dp', 'tensor')
- down_grad: float32 [2, 4096, 1024], P(None, 'tensor', 'dp')
- gains_grad: float32 [2, 2, 1024], P(None, None, ('dp', 'tensor'))
- biases_grad: float32 [2, 6, 1024], P(None, None, ('dp', 'tensor'))
- ff_bias_grad: float32 [2, 4096], P(None, ('dp', 'tensor'))
Inputs may be any that keep to these rules, and one draw needn't show every extreme that they name: `seg_ids`: within each sequence the document numbers never fall, and each document has 1 to 384 positions.
All inputs are finite; a program needn't handle non-finite values.
Results may differ from a plain program's by a relative error of at most 0.035.
Values may be sent and summed in bfloat16 or wider, within the bound.
No kernel may reach another device: no remote copies, remote signals or barrier semaphores. Data moves between devices by JAX's collectives and lax.ppermute only.
A program may use at most 256 MiB of HBM per device.

v0:
```python
from functools import partial
import jax
import jax.numpy as jnp
from jax import lax
from jax.sharding import PartitionSpec as P

HD = 64
EPSILON = 1e-06
HALF_ROOT = 0.7071067811865476
INV_ROOT_TAU = 0.3989422804014327


def normed(summed, gain_row, shift_row):
    centre = summed - jnp.mean(summed, axis=-1, keepdims=True)
    spread = jnp.mean(centre * centre, axis=-1, keepdims=True)
    return centre * lax.rsqrt(spread + EPSILON) * gain_row + shift_row


def gelu_slope(hidden_in):
    return (
        0.5 * (1.0 + lax.erf(hidden_in * HALF_ROOT))
        + hidden_in * jnp.exp(-0.5 * hidden_in * hidden_in) * INV_ROOT_TAU
    )


def collect(local_rows):
    return lax.all_gather(local_rows, "tensor", axis=0, tiled=True)


def reduce_rows(term_fn, row_count):
    return lax.psum_scatter(
        term_fn(jnp.int32(0), row_count * lax.axis_size("tensor")).astype(jnp.bfloat16),
        "tensor",
        scatter_dimension=0,
        tiled=True,
    ).astype(jnp.float32)


def project(operand, matrix, first_row, row_span):
    return jnp.dot(operand, matrix, preferred_element_type=jnp.float32)


def project_back(operand, matrix, first_row, row_span):
    return jnp.einsum("rf,df->rd", operand, matrix, preferred_element_type=jnp.float32)


def project_triple(operand, matrix, first_row, row_span):
    return jnp.einsum("rkc,kdc->rd", operand, matrix, preferred_element_type=jnp.float32)


def split_heads(matrix):
    return matrix.reshape(matrix.shape[0], matrix.shape[1] // HD, HD)


def masked_scores(query_heads, key_heads, segment):
    scores = jnp.einsum(
        "qhe,khe->hqk", query_heads, key_heads, preferred_element_type=jnp.float32
    ) * HD ** (-0.5)
    same_doc = segment[:, None] == segment[None, :]
    return jnp.where(same_doc[None], scores, -jnp.inf)


def attend_block(pieces):
    queries, key_rows, values, segment = pieces
    scores = masked_scores(split_heads(queries), split_heads(key_rows), segment)
    row_max = jnp.max(scores, axis=-1, keepdims=True)
    exp_scores = jnp.exp(scores - row_max)
    exp_total = jnp.sum(exp_scores, axis=-1, keepdims=True)
    attn_probs = (exp_scores / exp_total).astype(jnp.bfloat16)
    mixture = jnp.einsum(
        "hqk,khe->qhe", attn_probs, split_heads(values), preferred_element_type=jnp.float32
    )
    return (
        mixture.reshape(queries.shape).astype(jnp.bfloat16),
        (row_max + jnp.log(exp_total))[..., 0],
    )


def attend_back(pieces):
    queries, key_rows, values, segment, grad_mix, logsum = pieces
    query_heads = split_heads(queries)
    key_heads = split_heads(key_rows)
    value_heads = split_heads(values)
    grad_heads = split_heads(grad_mix)
    attn_probs = jnp.exp(masked_scores(query_heads, key_heads, segment) - logsum[..., None])
    grad_values = jnp.einsum(
        "hqk,qhe->khe",
        attn_probs.astype(jnp.bfloat16),
        grad_heads,
        preferred_element_type=jnp.float32,
    )
    grad_probs = jnp.einsum(
        "qhe,khe->hqk", grad_heads, value_heads, preferred_element_type=jnp.float32
    )
    inner_sum = jnp.sum(grad_probs * attn_probs, axis=-1, keepdims=True)
    grad_scores = (attn_probs * (grad_probs - inner_sum)).astype(jnp.bfloat16)
    grad_queries = jnp.einsum(
        "hqk,khe->qhe", grad_scores, key_heads, preferred_element_type=jnp.float32
    ) * HD ** (-0.5)
    grad_keys = jnp.einsum(
        "hqk,qhe->khe", grad_scores, query_heads, preferred_element_type=jnp.float32
    ) * HD ** (-0.5)
    stacked = jnp.stack([grad_queries, grad_keys, grad_values], axis=1)
    return stacked.reshape(queries.shape[0], 3, queries.shape[1]).astype(jnp.bfloat16)


def on_device(
    inputs,
    seg_ids,
    qkv_weight,
    out_weight,
    up_weight,
    down_weight,
    norm_gains,
    row_biases,
    ff_bias,
    cotangent,
):
    gain_rows, shift_rows, up_shifts = (
        lax.all_gather(norm_gains, ("dp", "tensor"), axis=2, tiled=True),
        lax.all_gather(row_biases, ("dp", "tensor"), axis=2, tiled=True),
        lax.all_gather(ff_bias, ("dp", "tensor"), axis=1, tiled=True),
    )
    tensor_rank = lax.axis_index("tensor")
    row_count = inputs.shape[0]
    model_width = inputs.shape[1]
    seq_count, length = seg_ids.shape
    head_cols = qkv_weight.shape[3]
    hidden = up_weight.shape[2]
    full_hidden = up_shifts.shape[1]
    layers = qkv_weight.shape[0]
    stream = inputs.astype(jnp.float32)
    stored = []
    for layer_index in range(layers):
        qkv_mat, out_mat, up_mat, down_mat = (
            lax.all_gather(qkv_weight[layer_index].astype(jnp.bfloat16), "dp", axis=1, tiled=True),
            lax.all_gather(out_weight[layer_index].astype(jnp.bfloat16), "dp", axis=1, tiled=True),
            lax.all_gather(up_weight[layer_index].astype(jnp.bfloat16), "dp", axis=0, tiled=True),
            lax.all_gather(down_weight[layer_index].astype(jnp.bfloat16), "dp", axis=1, tiled=True),
        )
        shifts = shift_rows[layer_index]
        query_shift = lax.dynamic_slice_in_dim(shifts[0], tensor_rank * head_cols, head_cols)
        value_shift = lax.dynamic_slice_in_dim(shifts[1], tensor_rank * head_cols, head_cols)
        up_shift = lax.dynamic_slice_in_dim(up_shifts[layer_index], tensor_rank * hidden, hidden)
        gathered = collect(stream.astype(jnp.bfloat16))
        projected = jnp.einsum("rd,kdc->rkc", gathered, qkv_mat, preferred_element_type=jnp.float32)
        projected = (
            projected + jnp.stack([query_shift, jnp.zeros_like(query_shift), value_shift])
        ).astype(jnp.bfloat16)
        by_sequence = projected.reshape(seq_count, length, 3, head_cols)
        mixture, logsum = lax.map(
            attend_block,
            (by_sequence[:, :, 0], by_sequence[:, :, 1], by_sequence[:, :, 2], seg_ids),
        )
        mixture = mixture.reshape(seq_count * length, head_cols)
        attended = reduce_rows(partial(project, mixture, out_mat), row_count)
        first_sum = stream + (attended + shifts[2])
        normed_mid = normed(first_sum, gain_rows[layer_index, 0], shifts[3])
        gathered_mid = collect(normed_mid.astype(jnp.bfloat16))
        hidden_in = jnp.dot(gathered_mid, up_mat, preferred_element_type=jnp.float32) + up_shift
        hidden_out = jax.nn.gelu(hidden_in, approximate=False).astype(jnp.bfloat16)
        branch_out = reduce_rows(partial(project, hidden_out, down_mat), row_count)
        second_sum = normed_mid + (branch_out + shifts[4])
        stream = normed(second_sum, gain_rows[layer_index, 1], shifts[5])
        stored.append(
            (
                qkv_mat,
                out_mat,
                up_mat,
                down_mat,
                gathered,
                projected,
                logsum,
                mixture,
                first_sum,
                gathered_mid,
                hidden_in,
                hidden_out,
                second_sum,
            )
        )
    grad_stream = cotangent
    weight_grads = [None] * layers
    small_grads = [None] * layers
    for layer_index in reversed(range(layers)):
        (
            qkv_mat,
            out_mat,
            up_mat,
            down_mat,
            gathered,
            projected,
            logsum,
            mixture,
            first_sum,
            gathered_mid,
            hidden_in,
            hidden_out,
            second_sum,
        ) = stored[layer_index]
        qkv_mat, out_mat, up_mat, down_mat = (
            lax.all_gather(qkv_weight[layer_index].astype(jnp.bfloat16), "dp", axis=1, tiled=True),
            lax.all_gather(out_weight[layer_index].astype(jnp.bfloat16), "dp", axis=1, tiled=True),
            lax.all_gather(up_weight[layer_index].astype(jnp.bfloat16), "dp", axis=0, tiled=True),
            lax.all_gather(down_weight[layer_index].astype(jnp.bfloat16), "dp", axis=1, tiled=True),
        )
        shifts = shift_rows[layer_index]
        layer_gains = gain_rows[layer_index]
        grad_second, grad_gain_late, grad_shift_late = jax.vjp(
            normed, second_sum, layer_gains[1], shifts[5]
        )[1](grad_stream)
        grad_branch = collect(grad_second.astype(jnp.bfloat16))
        grad_down = jnp.einsum(
            "rf,rd->fd", hidden_out, grad_branch, preferred_element_type=jnp.float32
        )
        grad_hidden = jnp.einsum(
            "rd,fd->rf", grad_branch, down_mat, preferred_element_type=jnp.float32
        )
        grad_pre = (grad_hidden * gelu_slope(hidden_in)).astype(jnp.bfloat16)
        grad_up = jnp.einsum(
            "rd,rf->df", gathered_mid, grad_pre, preferred_element_type=jnp.float32
        )
        grad_mid = grad_second + reduce_rows(partial(project_back, grad_pre, up_mat), row_count)
        grad_first, grad_gain_early, grad_shift_early = jax.vjp(
            normed, first_sum, layer_gains[0], shifts[3]
        )[1](grad_mid)
        grad_attn = collect(grad_first.astype(jnp.bfloat16))
        grad_out = jnp.einsum("rc,rd->cd", mixture, grad_attn, preferred_element_type=jnp.float32)
        grad_mix = jnp.einsum(
            "rd,cd->rc", grad_attn, out_mat, preferred_element_type=jnp.float32
        ).astype(jnp.bfloat16)
        by_sequence = projected.reshape(seq_count, length, 3, head_cols)
        grad_proj = lax.map(
            attend_back,
            (
                by_sequence[:, :, 0],
                by_sequence[:, :, 1],
                by_sequence[:, :, 2],
                seg_ids,
                grad_mix.reshape(seq_count, length, head_cols),
                logsum,
            ),
        )
        grad_proj = grad_proj.reshape(seq_count * length, 3, head_cols)
        grad_qkv = jnp.einsum(
            "rd,rkc->kdc", gathered, grad_proj, preferred_element_type=jnp.float32
        )
        grad_stream = grad_first + reduce_rows(
            partial(project_triple, grad_proj, qkv_mat), row_count
        )
        proj_sums = jnp.sum(grad_proj.astype(jnp.float32), axis=0)
        zero_row = jnp.zeros((model_width,), jnp.float32)
        grad_query_shift = lax.dynamic_update_slice_in_dim(
            zero_row, proj_sums[0], tensor_rank * head_cols, 0
        )
        grad_value_shift = lax.dynamic_update_slice_in_dim(
            zero_row, proj_sums[2], tensor_rank * head_cols, 0
        )
        grad_up_shift = lax.dynamic_update_slice_in_dim(
            jnp.zeros((full_hidden,), jnp.float32),
            jnp.sum(grad_pre.astype(jnp.float32), axis=0),
            tensor_rank * hidden,
            0,
        )
        small_grads[layer_index] = (
            jnp.stack([grad_gain_early, grad_gain_late]),
            jnp.stack(
                [
                    grad_query_shift,
                    grad_value_shift,
                    jnp.sum(grad_first, axis=0),
                    grad_shift_early,
                    jnp.sum(grad_second, axis=0),
                    grad_shift_late,
                ]
            ),
            grad_up_shift,
        )
        weight_grads[layer_index] = (
            lax.psum_scatter(
                grad_qkv.astype(jnp.bfloat16), "dp", scatter_dimension=1, tiled=True
            ).astype(jnp.float32),
            lax.psum_scatter(
                grad_out.astype(jnp.bfloat16), "dp", scatter_dimension=1, tiled=True
            ).astype(jnp.float32),
            lax.psum_scatter(
                grad_up.astype(jnp.bfloat16), "dp", scatter_dimension=0, tiled=True
            ).astype(jnp.float32),
            lax.psum_scatter(
                grad_down.astype(jnp.bfloat16), "dp", scatter_dimension=1, tiled=True
            ).astype(jnp.float32),
        )
    qkv_stack = jnp.stack([weight_grads[layer_index][0] for layer_index in range(layers)])
    out_stack = jnp.stack([weight_grads[layer_index][1] for layer_index in range(layers)])
    up_stack = jnp.stack([weight_grads[layer_index][2] for layer_index in range(layers)])
    down_stack = jnp.stack([weight_grads[layer_index][3] for layer_index in range(layers)])
    gains_all = jnp.stack([small_grads[layer_index][0] for layer_index in range(layers)])
    shifts_all = jnp.stack([small_grads[layer_index][1] for layer_index in range(layers)])
    hidden_all = jnp.stack([small_grads[layer_index][2] for layer_index in range(layers)])
    gains_grad, biases_grad, ff_bias_grad = (
        lax.psum_scatter(gains_all, ("dp", "tensor"), scatter_dimension=2, tiled=True),
        lax.psum_scatter(shifts_all, ("dp", "tensor"), scatter_dimension=2, tiled=True),
        lax.psum_scatter(hidden_all, ("dp", "tensor"), scatter_dimension=1, tiled=True),
    )
    return (
        stream.astype(jnp.bfloat16),
        grad_stream,
        qkv_stack,
        out_stack,
        up_stack,
        down_stack,
        gains_grad,
        biases_grad,
        ff_bias_grad,
    )


def solution(mesh):
    placed = (
        P(("dp", "tensor"), None),
        P("dp", None),
        P(None, None, "dp", "tensor"),
        P(None, "tensor", "dp"),
        P(None, "dp", "tensor"),
        P(None, "tensor", "dp"),
        P(None, None, ("dp", "tensor")),
        P(None, None, ("dp", "tensor")),
        P(None, ("dp", "tensor")),
        P(("dp", "tensor"), None),
    )
    return jax.shard_map(
        on_device,
        mesh=mesh,
        in_specs=placed,
        out_specs=(
            P(("dp", "tensor"), None),
            P(("dp", "tensor"), None),
            P(None, None, "dp", "tensor"),
            P(None, "tensor", "dp"),
            P(None, "dp", "tensor"),
            P(None, "tensor", "dp"),
            P(None, None, ("dp", "tensor")),
            P(None, None, ("dp", "tensor")),
            P(None, ("dp", "tensor")),
        ),
        check_vma=False,
    )
```

profile of v0, /device:TPU:0, one launch (start us, length us, event | category | flops | bytes accessed | tf_op | source)
XLA Modules:
  0.0 2121.0 jit_solution(10846130051365599466)
XLA Ops:
  12.5 79.0 %all_gather.67 = f32[2,6,1024]{1,0,2:T(2,128)S(1)} all-gather(f32[2,6,32]{1,0,2:T(2,128)S(1)} %copy.99), channel_id=1, replica_groups=mesh['dp'=16,'tensor'=2] {'dp','tensor'}, dimensions={2}, use_global_device_ids=true | all-gather | bytes 50688 | tf_op jit(solution)/shard_map/all_gather | solution.py:121
  91.5 27.6 %fusion.141 = (f32[1,1,1024]{1,0,2:T(1,128)S(1)}, f32[1,1,1024]{1,0,2:T(1,128)S(1)}, f32[1,1,1024]{1,0,2:T(1,128)S(1)}, f32[1024]{0:T(1024)S(1)}, f32[1024]{0:T(...) fusion(f32[2,6,1024]{1,0,2:T(2,128)S(1)} %all_gather.67), kind=kLoop, calls=%fused_computation.290 | loop fusion | bytes 98304 | tf_op jit(solution)/shard_map/slice | solution.py:142
  135.7 16.5 while.44
  158.6 72.7 %all_gather.69 = f32[2,2,1024]{1,0,2:T(2,128)S(1)} all-gather(f32[2,2,32]{1,0,2:T(2,128)S(1)} %copy.104), channel_id=1, replica_groups=mesh['dp'=16,'tensor'=2] {'dp','tensor'}, dimensions={2}, use_global_device_ids=true | all-gather | bytes 16896 | tf_op jit(solution)/shard_map/all_gather | solution.py:120
  231.3 26.9 %slice_reduce_fusion.1 = (f32[1024]{0:T(1024)}, f32[1024]{0:T(1024)}, f32[1024]{0:T(1024)S(1)}, f32[1024]{0:T(1024)S(1)}) fusion(f32[2,2,1024]{1,0,2:T(2,128)S(1)} %all_gather.69), kind=kLoop, calls=%fused_computation.222 | loop fusion | bytes 32768 | tf_op jit(solution)/shard_map/slice | solution.py:164
  264.5 65.2 %all_gather.72 = f32[2,4096]{1,0:T(2,128)S(1)} all-gather(f32[2,128]{1,0:T(2,128)S(1)} %copy-done.89), channel_id=1, replica_groups=mesh['dp'=16,'tensor'=2] {'dp','tensor'}, dimensions={1}, use_global_device_ids=true | all-gather | bytes 33792 | tf_op jit(solution)/shard_map/all_gather | solution.py:122
  330.3 25.8 %fusion.36 = (bf16[1024,2048]{1,0:T(8,128)(2,1)}, f32[1024,2048]{1,0:T(8,128)}) fusion(f32[2048]{0:T(1024)S(1)} %bitcast.432, bf16[1024,1024]{1,0:T(8,128)(2,1)} %all-gather.27.cloned.1.call-done, bf16[1,1024,2048]{2,1,0:T(8,128)(2,1)} %all-gather.45.cloned.1.call-done), kind=kOutput, calls=%fused_computation.80 | convolution fusion | flops 4433379328 | bytes 18882560 | tf_op jit(solution)/shard_map/dot_general | solution.py:160
  356.1 9.3 fusion.107
  366.3 27.6 %reduce-scatter.26.cloned.1.call-done = bf16[512,1024]{1,0:T(8,128)(2,1)} async-done(((bf16[1024,1024]{1,0:T(8,128)(2,1)}), bf16[512,1024]{1,0:T(8,128)(2,1)}) %reduce-scatter.26.cloned.1.call-update) | async-done | bytes 1048592 | tf_op jit(solution)/shard_map/reduce_scatter | solution.py:31
  399.8 41.4 %all-gather.49.cloned.1.call-done = bf16[1,3,1024,512]{3,2,1,0:T(8,128)(2,1)} async-done(((bf16[1,3,64,512]{3,2,1,0:T(8,128)(2,1)}), bf16[1,3,1024,512]{3,2,1,0:T(8,128)(2,1)}) %all-gather.49.cloned.1.call-update) | async-done | bytes 3145744 | tf_op jit(solution)/shard_map/all_gather | solution.py:136
  441.3 33.9 %all-gather.29.cloned.1.call-done = bf16[1024,1024]{1,0:T(8,128)(2,1)} async-done(((bf16[512,1024]{1,0:T(8,128)(2,1)}), bf16[1024,1024]{1,0:T(8,128)(2,1)}) %all-gather.29.cloned.1.call-update) | async-done | bytes 2097168 | tf_op jit(solution)/shard_map/all_gather | solution.py:27
  486.8 16.4 while.45
  503.3 12.0 all-gather.51.cloned.1.call-done
  520.3 30.1 %reduce-scatter.28.cloned.1.call-done = bf16[512,1024]{1,0:T(8,128)(2,1)} async-done(((bf16[1024,1024]{1,0:T(8,128)(2,1)}), bf16[512,1024]{1,0:T(8,128)(2,1)}) %reduce-scatter.28.cloned.1.call-update) | async-done | bytes 1048592 | tf_op jit(solution)/shard_map/reduce_scatter | solution.py:31
  556.0 48.1 %all-gather.53.cloned.1.call-done = bf16[1,1024,2048]{2,1,0:T(8,128)(2,1)} async-done(((bf16[1,64,2048]{2,1,0:T(8,128)(2,1)}), bf16[1,1024,2048]{2,1,0:T(8,128)(2,1)}) %all-gather.53.cloned.1.call-update) | async-done | bytes 4194320 | tf_op jit(solution)/shard_map/all_gather | solution.py:138
  604.1 33.7 %all-gather.31.cloned.1.call-done = bf16[1024,1024]{1,0:T(8,128)(2,1)} async-done(((bf16[512,1024]{1,0:T(8,128)(2,1)}), bf16[1024,1024]{1,0:T(8,128)(2,1)}) %all-gather.31.cloned.1.call-update) | async-done | bytes 2097168 | tf_op jit(solution)/shard_map/all_gather | solution.py:27
  637.8 25.6 %fusion.39 = (bf16[1024,2048]{1,0:T(8,128)(2,1)}, f32[1024,2048]{1,0:T(8,128)}) fusion(f32[2048]{0:T(1024)S(1)} %bitcast.435, bf16[1024,1024]{1,0:T(8,128)(2,1)} %all-gather.31.cloned.1.call-done, bf16[1,1024,2048]{2,1,0:T(8,128)(2,1)} %all-gather.53.cloned.1.call-done), kind=kOutput, calls=%fused_computation.83 | convolution fusion | flops 4433379328 | bytes 18882560 | tf_op jit(solution)/shard_map/dot_general | solution.py:160
  663.4 27.4 %all-gather.55.cloned.1.call-done = bf16[1,2048,1024]{1,2,0:T(8,128)(2,1)} async-done(((bf16[1,2048,64]{1,2,0:T(8,128)(2,1)}), bf16[1,2048,1024]{1,2,0:T(8,128)(2,1)}) %all-gather.55.cloned.1.call-update) | async-done | bytes 4194320 | tf_op jit(solution)/shard_map/all_gather | solution.py:139
  690.8 9.3 fusion.113
  700.2 30.4 %reduce-scatter.30.cloned.1.call-done = bf16[512,1024]{1,0:T(8,128)(2,1)} async-done(((bf16[1024,1024]{1,0:T(8,128)(2,1)}), bf16[512,1024]{1,0:T(8,128)(2,1)}) %reduce-scatter.30.cloned.1.call-update) | async-done | bytes 1048592 | tf_op jit(solution)/shard_map/reduce_scatter | solution.py:31
  739.1 33.0 %all-gather.33.cloned.1.call-done = bf16[1024,1024]{1,0:T(8,128)(2,1)} async-done(((bf16[512,1024]{1,0:T(8,128)(2,1)}), bf16[1024,1024]{1,0:T(8,128)(2,1)}) %all-gather.33.cloned.1.call-update) | async-done | bytes 2097168 | tf_op jit(solution)/shard_map/all_gather | solution.py:27
  772.1 11.4 convert_reduce_fusion
  791.3 31.9 %reduce-scatter.32.cloned.1.call-done = bf16[512,1024]{1,0:T(8,128)(2,1)} async-done(((bf16[1024,1024]{1,0:T(8,128)(2,1)}), bf16[512,1024]{1,0:T(8,128)(2,1)}) %reduce-scatter.32.cloned.1.call-update) | async-done | bytes 1048592 | tf_op jit(solution)/shard_map/reduce_scatter | solution.py:31
  830.7 33.0 %all-gather.35.cloned.1.call-done = bf16[1024,1024]{1,0:T(8,128)(2,1)} async-done(((bf16[512,1024]{1,0:T(8,128)(2,1)}), bf16[1024,1024]{1,0:T(8,128)(2,1)}) %all-gather.35.cloned.1.call-update) | async-done | bytes 2097168 | tf_op jit(solution)/shard_map/all_gather | solution.py:27
  869.4 32.0 %while.46 = (s32[]{:T(128)}, bf16[2,512,3,512]{1,3,2,0:T(8,128)(2,1)}, bf16[2,512,512]{1,2,0:T(8,128)(2,1)S(1)}, s32[2,512]{1,0:T(2,128)S(1)}, bf16[2,512,512]{1...) while((s32[]{:T(128)}, ...), condition=%wide.region_27.28_spmd, body=%wide.region_25.27_spmd.sunk | while | flops 1379921920 | bytes 102881448 | solution.py:233
  906.0 7.7 bitcast_convert_fusion.1
  914.3 31.5 %reduce-scatter.34.cloned.1.call-done = bf16[512,1024]{1,0:T(8,128)(2,1)} async-done(((bf16[1024,1024]{1,0:T(8,128)(2,1)}), bf16[512,1024]{1,0:T(8,128)(2,1)}) %reduce-scatter.34.cloned.1.call-update) | async-done | bytes 1048592 | tf_op jit(solution)/shard_map/reduce_scatter | solution.py:31
  953.0 33.2 %all-gather.37.cloned.1.call-done = bf16[1024,1024]{1,0:T(8,128)(2,1)} async-done(((bf16[512,1024]{1,0:T(8,128)(2,1)}), bf16[1024,1024]{1,0:T(8,128)(2,1)}) %all-gather.37.cloned.1.call-update) | async-done | bytes 2097168 | tf_op jit(solution)/shard_map/all_gather | solution.py:27
  986.3 10.8 convert_reduce_fusion.1
  1004.9 31.9 %reduce-scatter.36.cloned.1.call-done = bf16[512,1024]{1,0:T(8,128)(2,1)} async-done(((bf16[1024,1024]{1,0:T(8,128)(2,1)}), bf16[512,1024]{1,0:T(8,128)(2,1)}) %reduce-scatter.36.cloned.1.call-update) | async-done | bytes 1048592 | tf_op jit(solution)/shard_map/reduce_scatter | solution.py:31
  1049.9 9.8 convolution_convert_fusion
  1061.3 8.3 convolution_convert_fusion.1
  1071.2 8.4 convolution_convert_fusion.2
  1082.1 9.4 convolution_convert_fusion.3
  1098.5 32.0 %while.47 = (s32[]{:T(128)}, bf16[2,512,3,512]{1,3,2,0:T(8,128)(2,1)}, bf16[2,512,512]{1,2,0:T(8,128)(2,1)S(1)}, s32[2,512]{1,0:T(2,128)S(1)}, bf16[2,512,512]{1...) while((s32[]{:T(128)}, ...), condition=%wide.region_36.37_spmd, body=%wide.region_34.36_spmd.sunk | while | flops 1379921920 | bytes 102881448 | solution.py:233
  1150.3 7.8 copy.116
  1174.6 6.5 bitcast_convert_fusion
  1182.4 35.2 %reduce-scatter.56.cloned.1.call-done = f32[128,2]{1,0:T(8,128)} async-done(((f32[4096,2]{1,0:T(8,128)}), f32[128,2]{1,0:T(8,128)}) %reduce-scatter.56.cloned.1.call-update) | async-done | bytes 1040
  1219.1 132.1 %reduce-scatter.52.cloned.1.call-done = f32[32,4]{1,0:T(8,128)} async-done(((f32[1024,4]{1,0:T(8,128)}), f32[32,4]{1,0:T(8,128)}) %reduce-scatter.52.cloned.1.call-update) | async-done | bytes 528
  1352.6 71.4 %reduce-scatter.50.cloned.1.call-done = bf16[2048,64]{0,1:T(8,128)(2,1)} async-done(((bf16[2048,1024]{0,1:T(8,128)(2,1)}), bf16[2048,64]{0,1:T(8,128)(2,1)}) %reduce-scatter.50.cloned.1.call-update) | async-done | bytes 262160 | tf_op jit(solution)/shard_map/reduce_scatter | solution.py:289
  1424.1 75.1 %reduce-scatter.48.cloned.1.call-done = bf16[2048,64]{0,1:T(8,128)(2,1)} async-done(((bf16[2048,1024]{0,1:T(8,128)(2,1)}), bf16[2048,64]{0,1:T(8,128)(2,1)}) %reduce-scatter.48.cloned.1.call-update) | async-done | bytes 262160 | tf_op jit(solution)/shard_map/reduce_scatter | solution.py:289
  1501.2 74.2 %reduce-scatter.46.cloned.1.call-done = bf16[64,2048]{1,0:T(8,128)(2,1)} async-done(((bf16[1024,2048]{1,0:T(8,128)(2,1)}), bf16[64,2048]{1,0:T(8,128)(2,1)}) %reduce-scatter.46.cloned.1.call-update) | async-done | bytes 262160 | tf_op jit(solution)/shard_map/reduce_scatter | solution.py:286
  1575.4 75.4 %reduce-scatter.44.cloned.1.call-done = bf16[64,2048]{1,0:T(8,128)(2,1)} async-done(((bf16[1024,2048]{1,0:T(8,128)(2,1)}), bf16[64,2048]{1,0:T(8,128)(2,1)}) %reduce-scatter.44.cloned.1.call-update) | async-done | bytes 262160 | tf_op jit(solution)/shard_map/reduce_scatter | solution.py:286
  1652.9 132.9 %reduce-scatter.54.cloned.1.call-done = f32[32,12]{1,0:T(8,128)} async-done(((f32[1024,12]{1,0:T(8,128)}), f32[32,12]{1,0:T(8,128)}) %reduce-scatter.54.cloned.1.call-update) | async-done | bytes 1552
  1787.2 55.5 %reduce-scatter.42.cloned.1.call-done = bf16[512,64]{0,1:T(8,128)(2,1)} async-done(((bf16[512,1024]{0,1:T(8,128)(2,1)}), bf16[512,64]{0,1:T(8,128)(2,1)}) %reduce-scatter.42.cloned.1.call-update) | async-done | bytes 65552 | tf_op jit(solution)/shard_map/reduce_scatter | solution.py:283
  1842.8 60.6 %reduce-scatter.40.cloned.1.call-done = bf16[512,64]{0,1:T(8,128)(2,1)} async-done(((bf16[512,1024]{0,1:T(8,128)(2,1)}), bf16[512,64]{0,1:T(8,128)(2,1)}) %reduce-scatter.40.cloned.1.call-update) | async-done | bytes 65552 | tf_op jit(solution)/shard_map/reduce_scatter | solution.py:283
  1905.0 171.3 %all-reduce.5.cloned.1.call-done = (bf16[3,1024,512]{2,0,1:T(4,128)(2,1)}, bf16[3,1024,512]{2,0,1:T(4,128)(2,1)}) async-done(((bf16[3,1024,512]{2,0,1:T(4,128)(2,1)}, bf16[3,1024,512]{2,0,1:T(4,128)(2,1)}), (bf16[3,1024,512]{2,0,1:T(4,128)(2,1)}, bf16[3,1024,512]{2,0,1:T(4,128)(2,1)})) %all-reduce.5.cloned.1.call-update) | async-done | bytes 6291472
  2079.9 31.1 %reduce-scatter.38.cloned.1.call-done = bf16[512,1024]{1,0:T(8,128)(2,1)} async-done(((bf16[1024,1024]{1,0:T(8,128)(2,1)}), bf16[512,1024]{1,0:T(8,128)(2,1)}) %reduce-scatter.38.cloned.1.call-update) | async-done | bytes 1048592 | tf_op jit(solution)/shard_map/reduce_scatter | solution.py:31
  (503 shorter events, 288.2 us)
Async XLA Ops:
  7.2 116.7 %all-gather.25.cloned.1.call-start = ((), (), s32[]{:S(2)}) async-start(), calls=%async_computation.17 | async-start | bytes 3145728 | tf_op jit(solution)/shard_map/all_gather | solution.py:27
  7.9 116.0 %all-gather.41.cloned.1.call-start = ((), (), s32[]{:S(2)}) async-start(), calls=%async_computation.39 | async-start | bytes 3342336 | tf_op jit(solution)/shard_map/all_gather | solution.py:136
  9.9 142.3 %all-gather.43.cloned.1.call-start = ((), (), s32[]{:S(2)}) async-start(), calls=%async_computation.40 | async-start | bytes 1114112 | tf_op jit(solution)/shard_map/all_gather | solution.py:137
  11.6 246.6 %reduce-scatter.24.cloned.1.call-start = ((), (), s32[]{:S(2)}) async-start(), calls=%async_computation.18 | async-start | bytes 3145728 | tf_op jit(solution)/shard_map/reduce_scatter | solution.py:31
  119.1 274.7 %copy-start.44 = (f32[1024]{0:T(1024)}, f32[1024]{0:T(1024)S(1)}, u32[]{:S(2)}) copy-start(f32[1024]{0:T(1024)S(1)} %get-tuple-element.406) | copy-start | bytes 12292
  157.4 100.8 %copy-start.2 = (bf16[512,1024]{1,0:T(8,128)(2,1)S(1)}, bf16[512,1024]{1,0:T(8,128)(2,1)}, u32[]{:S(2)}) copy-start(bf16[512,1024]{1,0:T(8,128)(2,1)} %param.18) | copy-start | bytes 3145732
  157.4 172.9 %all-gather.45.cloned.1.call-start = ((), (), s32[]{:S(2)}) async-start(), calls=%async_computation.41 | async-start | bytes 4456448 | tf_op jit(solution)/shard_map/all_gather | solution.py:138
  158.4 171.9 %all-gather.27.cloned.1.call-start = ((), (), s32[]{:S(2)}) async-start(), calls=%async_computation.19 | async-start | bytes 3145728 | tf_op jit(solution)/shard_map/all_gather | solution.py:27
  258.2 135.6 %copy-start.49 = (f32[1024]{0:T(1024)}, f32[1024]{0:T(1024)S(1)}, u32[]{:S(2)}) copy-start(f32[1024]{0:T(1024)S(1)} %get-tuple-element.293) | copy-start | bytes 12292
  258.2 292.2 %copy-start.46 = (f32[1024]{0:T(1024)}, f32[1024]{0:T(1024)S(1)}, u32[]{:S(2)}) copy-start(f32[1024]{0:T(1024)S(1)} %get-tuple-element.292) | copy-start | bytes 12292
  260.0 133.8 %copy-start.53 = (f32[512]{0:T(512)}, f32[512]{0:T(512)S(1)}, u32[]{:S(2)}) copy-start(f32[512]{0:T(512)S(1)} %broadcast_multiply_fusion.3) | copy-start | bytes 6148
  261.8 94.2 %copy-start.65 = (f32[512]{0:T(512)}, f32[512]{0:T(512)S(1)}, u32[]{:S(2)}) copy-start(f32[512]{0:T(512)S(1)} %multiply_reduce_fusion.13) | copy-start | bytes 6148
  261.8 132.0 %copy-start.57 = (f32[512]{0:T(512)}, f32[512]{0:T(512)S(1)}, u32[]{:S(2)}) copy-start(f32[512]{0:T(512)S(1)} %fusion.125) | copy-start | bytes 6148
  263.5 92.6 %all-gather.47.cloned.1.call-start = ((), (), s32[]{:S(2)}) async-start(), calls=%async_computation.42 | async-start | bytes 4456448 | tf_op jit(solution)/shard_map/all_gather | solution.py:139
  264.4 129.4 %reduce-scatter.26.cloned.1.call-start = ((), (), s32[]{:S(2)}) async-start(), calls=%async_computation.20 | async-start | bytes 3145728 | tf_op jit(solution)/shard_map/reduce_scatter | solution.py:31
  365.5 75.8 %all-gather.49.cloned.1.call-start = ((), (), s32[]{:S(2)}) async-start(), calls=%async_computation.43 | async-start | bytes 3342336 | tf_op jit(solution)/shard_map/all_gather | solution.py:136
  366.2 109.0 %all-gather.29.cloned.1.call-start = ((), (), s32[]{:S(2)}) async-start(), calls=%async_computation.21 | async-start | bytes 3145728 | tf_op jit(solution)/shard_map/all_gather | solution.py:27
  396.1 79.1 %copy-start.84 = (f32[3,512]{1,0:T(4,128)S(1)}, f32[3,512]{1,0:T(4,128)}, u32[]{:S(2)}) copy-start(f32[3,512]{1,0:T(4,128)} %get-tuple-element.426) | copy-start | bytes 18436
  396.1 154.3 %copy-start.51 = (f32[512]{0:T(512)}, f32[512]{0:T(512)S(1)}, u32[]{:S(2)}) copy-start(f32[512]{0:T(512)S(1)} %broadcast_multiply_fusion.2) | copy-start | bytes 6148
  396.4 84.7 %copy-start.67 = (f32[512]{0:T(512)}, f32[512]{0:T(512)S(1)}, u32[]{:S(2)}) copy-start(f32[512]{0:T(512)S(1)} %multiply_reduce_fusion.12) | copy-start | bytes 6148
  396.5 154.0 %copy-start.55 = (f32[512]{0:T(512)}, f32[512]{0:T(512)S(1)}, u32[]{:S(2)}) copy-start(f32[512]{0:T(512)S(1)} %fusion.126) | copy-start | bytes 6148
  398.8 116.5 %all-gather.51.cloned.1.call-start = ((), (), s32[]{:S(2)}) async-start(), calls=%async_computation.44 | async-start | bytes 1114112 | tf_op jit(solution)/shard_map/all_gather | solution.py:137
  399.6 150.9 %reduce-scatter.28.cloned.1.call-start = ((), (), s32[]{:S(2)}) async-start(), calls=%async_computation.22 | async-start | bytes 3145728 | tf_op jit(solution)/shard_map/reduce_scatter | solution.py:31
  519.5 84.6 %all-gather.53.cloned.1.call-start = ((), (), s32[]{:S(2)}) async-start(), calls=%async_computation.45 | async-start | bytes 4456448 | tf_op jit(solution)/shard_map/all_gather | solution.py:138
  520.3 117.5 %all-gather.31.cloned.1.call-start = ((), (), s32[]{:S(2)}) async-start(), calls=%async_computation.23 | async-start | bytes 3145728 | tf_op jit(solution)/shard_map/all_gather | solution.py:27
  553.5 110.0 %copy-start.69 = (f32[512]{0:T(512)}, f32[512]{0:T(512)S(1)}, u32[]{:S(2)}) copy-start(f32[512]{0:T(512)S(1)} %multiply_reduce_fusion.11) | copy-start | bytes 6148
  554.9 135.9 %all-gather.55.cloned.1.call-start = ((), (), s32[]{:S(2)}) async-start(), calls=%async_computation.46 | async-start | bytes 4456448 | tf_op jit(solution)/shard_map/all_gather | solution.py:139
  555.5 175.1 %reduce-scatter.30.cloned.1.call-start = ((), (), s32[]{:S(2)}) async-start(), calls=%async_computation.24 | async-start | bytes 3145728 | tf_op jit(solution)/shard_map/reduce_scatter | solution.py:31
  700.2 72.0 %all-gather.33.cloned.1.call-start = ((), (), s32[]{:S(2)}) async-start(), calls=%async_computation.25 | async-start | bytes 3145728 | tf_op jit(solution)/shard_map/all_gather | solution.py:27
  738.9 84.3 %reduce-scatter.32.cloned.1.call-start = ((), (), s32[]{:S(2)}) async-start(), calls=%async_computation.26 | async-start | bytes 3145728 | tf_op jit(solution)/shard_map/reduce_scatter | solution.py:31
  791.2 72.4 %all-gather.35.cloned.1.call-start = ((), (), s32[]{:S(2)}) async-start(), calls=%async_computation.27 | async-start | bytes 3145728 | tf_op jit(solution)/shard_map/all_gather | solution.py:27
  830.4 115.4 %reduce-scatter.34.cloned.1.call-start = ((), (), s32[]{:S(2)}) async-start(), calls=%async_computation.28 | async-start | bytes 3145728 | tf_op jit(solution)/shard_map/reduce_scatter | solution.py:31
  913.8 72.5 %all-gather.37.cloned.1.call-start = ((), (), s32[]{:S(2)}) async-start(), calls=%async_computation.29 | async-start | bytes 3145728 | tf_op jit(solution)/shard_map/all_gather | solution.py:27
  953.0 83.8 %reduce-scatter.36.cloned.1.call-start = ((), (), s32[]{:S(2)}) async-start(), calls=%async_computation.30 | async-start | bytes 3145728 | tf_op jit(solution)/shard_map/reduce_scatter | solution.py:31
  1004.8 86.9 %all-gather.39.cloned.1.call-start = ((), (), s32[]{:S(2)}) async-start(), calls=%async_computation.31 | async-start | bytes 3145728 | tf_op jit(solution)/shard_map/all_gather | solution.py:27
  1045.3 172.3 %reduce-scatter.56.cloned.1.call-start = ((), (), s32[]{:S(2)}) async-start(), calls=%async_computation.49 | async-start | bytes 2162688
  1047.6 303.6 %reduce-scatter.52.cloned.1.call-start = ((), (), s32[]{:S(2)}) async-start(), calls=%async_computation.47 | async-start | bytes 540672
  1049.7 374.4 %reduce-scatter.50.cloned.1.call-start = ((), (), s32[]{:S(2)}) async-start(), calls=%async_computation.38 | async-start | bytes 4456448 | tf_op jit(solution)/shard_map/reduce_scatter | solution.py:289
  1059.8 439.4 %reduce-scatter.48.cloned.1.call-start = ((), (), s32[]{:S(2)}) async-start(), calls=%async_computation.37 | async-start | bytes 4456448 | tf_op jit(solution)/shard_map/reduce_scatter | solution.py:289
  1069.6 505.8 %reduce-scatter.46.cloned.1.call-start = ((), (), s32[]{:S(2)}) async-start(), calls=%async_computation.36 | async-start | bytes 4456448 | tf_op jit(solution)/shard_map/reduce_scatter | solution.py:286
  1079.6 571.2 %reduce-scatter.44.cloned.1.call-start = ((), (), s32[]{:S(2)}) async-start(), calls=%async_computation.35 | async-start | bytes 4456448 | tf_op jit(solution)/shard_map/reduce_scatter | solution.py:286
  1091.5 694.2 %reduce-scatter.54.cloned.1.call-start = ((), (), s32[]{:S(2)}) async-start(), calls=%async_computation.48 | async-start | bytes 540672
  1135.1 707.7 %reduce-scatter.42.cloned.1.call-start = ((), (), s32[]{:S(2)}) async-start(), calls=%async_computation.34 | async-start | bytes 1114112 | tf_op jit(solution)/shard_map/reduce_scatter | solution.py:283
  1139.0 764.3 %reduce-scatter.40.cloned.1.call-start = ((), (), s32[]{:S(2)}) async-start(), calls=%async_computation.33 | async-start | bytes 1114112 | tf_op jit(solution)/shard_map/reduce_scatter | solution.py:283
  1143.7 932.6 %all-reduce.5.cloned.1.call-start = ((), (), s32[]{:S(2)}) async-start(), calls=%async_computation.50 | async-start | bytes 16777216
  1172.7 938.2 %reduce-scatter.38.cloned.1.call-start = ((), (), s32[]{:S(2)}) async-start(), calls=%async_computation.32 | async-start | bytes 3145728 | tf_op jit(solution)/shard_map/reduce_scatter | solution.py:31
  1181.1 929.8 %copy-start.27 = (f32[512,1024]{1,0:T(8,128)S(1)}, f32[512,1024]{1,0:T(8,128)}, u32[]{:S(2)}) copy-start(f32[512,1024]{1,0:T(8,128)} %copy-done.26) | copy-start | bytes 6291460
  1181.1 929.8 %copy-start.64 = (f32[512]{0:T(512)S(1)}, f32[512]{0:T(512)}, u32[]{:S(2)}) copy-start(f32[512]{0:T(512)} %copy-done.63) | copy-start | bytes 6148
  (89 other events, 1391.8 us)
Sparse Core Ops, SparseCore 0:
  9.6 44.2 all-gather.24
  56.6 47.1 all-gather.40
  106.6 36.7 all-gather.42
  157.5 37.1 reduce-scatter.23
  197.5 50.7 all-gather.44
  263.6 30.7 all-gather.26
  297.3 50.5 all-gather.46
  365.6 28.1 reduce-scatter.25
  396.0 45.1 all-gather.48
  443.2 31.9 all-gather.28
  477.4 37.9 all-gather.50
  519.6 30.7 reduce-scatter.27
  553.4 50.6 all-gather.52
  606.2 31.6 all-gather.30
  640.1 50.7 all-gather.54
  700.3 30.3 reduce-scatter.29
  739.0 33.0 all-gather.32
  791.3 31.8 reduce-scatter.31
  830.5 33.1 all-gather.34
  913.9 31.8 reduce-scatter.33
  953.1 33.1 all-gather.36
  1005.0 31.8 reduce-scatter.35
  1045.5 33.1 all-gather.38
  1080.8 136.7 reduce-scatter.55
  1220.4 130.7 reduce-scatter.51
  1355.4 68.6 reduce-scatter.49
  1427.8 71.3 reduce-scatter.47
  1503.5 71.8 reduce-scatter.45
  1579.3 71.4 reduce-scatter.43
  1653.0 132.7 reduce-scatter.53
  1789.4 53.3 reduce-scatter.41
  1846.8 56.5 reduce-scatter.39
  1907.0 169.2 all-reduce.4
  2079.2 31.6 reduce-scatter.37
where the time goes:
time: 2130 us; the launch traced here: 2120 us
  waiting for transfers between devices  1400 us (66%)
  matrix products  253 us (12%)
  blocking collectives  217 us (10%)
  local copies, waits for them, and re-layouts  158 us (7%)
  other arithmetic  73.7 us (3%)
    unnamed x38, waiting for transfers between devices  475 us
    reduce_scatter x8, waiting for transfers between devices, reduce_rows(): lax.psum_scatter(term_fn(jnp.int32(0), row_count * lax.axis_size('tensor'...  214 us
    all_gather x8, waiting for transfers between devices, collect(): return lax.all_gather(local_rows, 'tensor', axis=0, tiled=True)  167 us
    reduce_scatter x2, waiting for transfers between devices, on_device(): lax.psum_scatter(grad_up.astype(jnp.bfloat16), 'dp', scatter_dimension=0,...  150 us
    reduce_scatter x2, waiting for transfers between devices, on_device(): lax.psum_scatter(grad_down.astype(jnp.bfloat16), 'dp', scatter_dimension=...  147 us
    reduce_scatter x2, waiting for transfers between devices, on_device(): lax.psum_scatter(grad_out.astype(jnp.bfloat16), 'dp', scatter_dimension=1...  116 us
    all_gather x1, blocking collectives, on_device(): lax.all_gather(row_biases, ('dp', 'tensor'), axis=2, tiled=True)  79 us
    all_gather x1, blocking collectives, on_device(): lax.all_gather(norm_gains, ('dp', 'tensor'), axis=2, tiled=True)  72.7 us
  transfers between devices with their start and end apart: 34, of which 26 were waited for; matrix products, arithmetic and copies ran while one was open for 15% of the time, Pallas kernels for 0%

commit v1 on v0

--- a/solution.py
+++ b/solution.py
@@ -8,6 +8,24 @@
 EPSILON = 1e-06
 HALF_ROOT = 0.7071067811865476
 INV_ROOT_TAU = 0.3989422804014327
+
+
+def collect_2(array, axis, dim):
+    ways, here, step = (lax.axis_size(axis), lax.axis_index(axis), array.shape[dim])
+    shape = [n * ways if d == dim else n for d, n in enumerate(array.shape)]
+    full = lax.dynamic_update_slice_in_dim(
+        jnp.zeros(shape, array.dtype), array, here * step, axis=dim
+    )
+    going_up = going_down = array
+    for far in range(1, ways // 2 + 1):
+        going_up = lax.ppermute(going_up, axis, [(d, (d + 1) % ways) for d in range(ways)])
+        full = lax.dynamic_update_slice_in_dim(full, going_up, (here - far) % ways * step, axis=dim)
+        if 2 * far < ways:
+            going_down = lax.ppermute(going_down, axis, [(d, (d - 1) % ways) for d in range(ways)])
+            full = lax.dynamic_update_slice_in_dim(
+                full, going_down, (here + far) % ways * step, axis=dim
+            )
+    return full
 
 
 def normed(summed, gain_row, shift_row):
@@ -135,7 +153,7 @@
         qkv_mat, out_mat, up_mat, down_mat = (
             lax.all_gather(qkv_weight[layer_index].astype(jnp.bfloat16), "dp", axis=1, tiled=True),
             lax.all_gather(out_weight[layer_index].astype(jnp.bfloat16), "dp", axis=1, tiled=True),
-            lax.all_gather(up_weight[layer_index].astype(jnp.bfloat16), "dp", axis=0, tiled=True),
+            collect_2(up_weight[layer_index].astype(jnp.bfloat16), "dp", 0),
             lax.all_gather(down_weight[layer_index].astype(jnp.bfloat16), "dp", axis=1, tiled=True),
         )
         shifts = shift_rows[layer_index]

time: 2130 us -> 2260 us (1.061)
  starting transfers between devices: 3.5 us -> 65.8 us
  matrix products: 253 us -> 282 us
    ppermute x0 -> x30, starting transfers between devices: none -> 62.4 us  [the longest x14 62.1 us: collect_2(): lax.ppermute(going_down, axis, [(d, (d - 1) % ways) for d in range(ways)])]
    ppermute x0 -> x30, waiting for transfers between devices: none -> 58.8 us  [the longest x16 58 us: collect_2(): lax.ppermute(going_up, axis, [(d, (d + 1) % ways) for d in range(ways)])]
    all_gather x8, waiting for transfers between devices: 167 us -> 132 us  [collect(): return lax.all_gather(local_rows, 'tensor', axis=0, tiled=True)]
    all_gather x2, waiting for transfers between devices: 48.1 us -> 81.7 us  [on_device(): lax.all_gather(up_weight[layer_index].astype(jnp.bfloat16), 'dp', axis=0,...]
    all_gather x2, waiting for transfers between devices: 27.4 us -> 0.01 us  [on_device(): lax.all_gather(down_weight[layer_index].astype(jnp.bfloat16), 'dp', axis=...]
    dynamic_update_slice x0 -> x32, local copies, waits for them, and re-layouts: none -> 23.1 us  [the longest x16 11.5 us: collect_2(): lax.dynamic_update_slice_in_dim(full, going_up, (here - far) % ways * ste...]
  transfers between devices with their start and end apart: 34 -> 64, of which waited for: 26 -> 41; matrix products, arithmetic and copies ran while one was open for 15% -> 17% of each run, Pallas kernels for 0% -> 0%
where the time goes in v1:
time: 2260 us; the launch traced here: 2250 us
  waiting for transfers between devices  1410 us (62%)
  matrix products  282 us (12%)
  blocking collectives  216 us (10%)
  local copies, waits for them, and re-layouts  177 us (8%)
  other arithmetic  82.6 us (4%)
  starting transfers between devices  65.8 us (3%)
    unnamed x38, waiting for transfers between devices  465 us
    reduce_scatter x8, waiting for transfers between devices, reduce_rows(): lax.psum_scatter(term_fn(jnp.int32(0), row_count * lax.axis_size('tensor'...  209 us
    reduce_scatter x2, waiting for transfers between devices, on_device(): lax.psum_scatter(grad_up.astype(jnp.bfloat16), 'dp', scatter_dimension=0,...  149 us
    reduce_scatter x2, waiting for transfers between devices, on_device(): lax.psum_scatter(grad_down.astype(jnp.bfloat16), 'dp', scatter_dimension=...  147 us
    all_gather x8, waiting for transfers between devices, collect(): return lax.all_gather(local_rows, 'tensor', axis=0, tiled=True)  132 us
    reduce_scatter x2, waiting for transfers between devices, on_device(): lax.psum_scatter(grad_out.astype(jnp.bfloat16), 'dp', scatter_dimension=1...  116 us
    all_gather x2, waiting for transfers between devices, on_device(): lax.all_gather(up_weight[layer_index].astype(jnp.bfloat16), 'dp', axis=0,...  81.7 us
    all_gather x1, blocking collectives, on_device(): lax.all_gather(row_biases, ('dp', 'tensor'), axis=2, tiled=True)  79 us
  transfers between devices with their start and end apart: 64, of which 41 were waited for; matrix products, arithmetic and copies ran while one was open for 17% of the time, Pallas kernels for 0%

profile of v1, /device:TPU:0, one launch (start us, length us, event | category | flops | bytes accessed | tf_op | source)
XLA Modules:
  0.0 2253.1 jit_solution(18301795725794424769)
XLA Ops:
  12.5 79.0 %all_gather.65 = f32[2,6,1024]{1,0,2:T(2,128)S(1)} all-gather(f32[2,6,32]{1,0,2:T(2,128)S(1)} %copy.99), channel_id=1, replica_groups=mesh['dp'=16,'tensor'=2] {'dp','tensor'}, dimensions={2}, use_global_device_ids=true | all-gather | bytes 50688 | tf_op jit(solution)/shard_map/all_gather | solution.py:139
  91.5 27.5 %fusion.137 = (f32[1,1,1024]{1,0,2:T(1,128)S(1)}, f32[1,1,1024]{1,0,2:T(1,128)S(1)}, f32[1,1,1024]{1,0,2:T(1,128)S(1)}, f32[1024]{0:T(1024)S(1)}, f32[1024]{0:T(...) fusion(f32[2,6,1024]{1,0,2:T(2,128)S(1)} %all_gather.65), kind=kLoop, calls=%fused_computation.320 | loop fusion | bytes 98304 | tf_op jit(solution)/shard_map/slice | solution.py:160
  134.7 17.3 while.44
  156.5 71.3 %all_gather.67 = f32[2,2,1024]{1,0,2:T(2,128)S(1)} all-gather(f32[2,2,32]{1,0,2:T(2,128)S(1)} %copy.104), channel_id=1, replica_groups=mesh['dp'=16,'tensor'=2] {'dp','tensor'}, dimensions={2}, use_global_device_ids=true | all-gather | bytes 16896 | tf_op jit(solution)/shard_map/all_gather | solution.py:138
  227.8 26.7 %slice_reduce_fusion.1 = (f32[1024]{0:T(1024)}, f32[1024]{0:T(1024)}, f32[1024]{0:T(1024)S(1)}, f32[1024]{0:T(1024)S(1)}) fusion(f32[2,2,1024]{1,0,2:T(2,128)S(1)} %all_gather.67), kind=kLoop, calls=%fused_computation.218 | loop fusion | bytes 32768 | tf_op jit(solution)/shard_map/slice | solution.py:182
  268.8 65.8 %all_gather.69 = f32[2,4096]{1,0:T(2,128)S(1)} all-gather(f32[2,128]{1,0:T(2,128)S(1)} %copy-done.80), channel_id=1, replica_groups=mesh['dp'=16,'tensor'=2] {'dp','tensor'}, dimensions={1}, use_global_device_ids=true | all-gather | bytes 33792 | tf_op jit(solution)/shard_map/all_gather | solution.py:140
  400.6 25.7 %fusion.36 = (bf16[1024,2048]{1,0:T(8,128)(2,1)}, f32[1024,2048]{1,0:T(8,128)}) fusion(f32[2048]{0:T(1024)S(1)} %bitcast.432, bf16[1024,1024]{1,0:T(8,128)(2,1)} %all-gather.27.cloned.1.call-done, bf16[1024,2048]{1,0:T(8,128)(2,1)} %constant_dynamic-update-slice_fusion.24), kind=kOutput, calls=%fused_computation.80 | convolution fusion | flops 4433379328 | bytes 18882560 | tf_op jit(solution)/shard_map/dot_general | solution.py:178
  426.3 9.3 fusion.100
  436.5 27.1 %reduce-scatter.26.cloned.1.call-done = bf16[512,1024]{1,0:T(8,128)(2,1)} async-done(((bf16[1024,1024]{1,0:T(8,128)(2,1)}), bf16[512,1024]{1,0:T(8,128)(2,1)}) %reduce-scatter.26.cloned.1.call-update) | async-done | bytes 1048592 | tf_op jit(solution)/shard_map/reduce_scatter | solution.py:49
  469.5 41.4 %all-gather.47.cloned.1.call-done = bf16[1,3,1024,512]{3,2,1,0:T(8,128)(2,1)} async-done(((bf16[1,3,64,512]{3,2,1,0:T(8,128)(2,1)}), bf16[1,3,1024,512]{3,2,1,0:T(8,128)(2,1)}) %all-gather.47.cloned.1.call-update) | async-done | bytes 3145744 | tf_op jit(solution)/shard_map/all_gather | solution.py:154
  511.0 34.1 %all-gather.29.cloned.1.call-done = bf16[1024,1024]{1,0:T(8,128)(2,1)} async-done(((bf16[512,1024]{1,0:T(8,128)(2,1)}), bf16[1024,1024]{1,0:T(8,128)(2,1)}) %all-gather.29.cloned.1.call-update) | async-done | bytes 2097168 | tf_op jit(solution)/shard_map/all_gather | solution.py:45
  555.5 17.3 while.45
  572.8 12.3 all-gather.49.cloned.1.call-done
  589.0 30.8 %reduce-scatter.28.cloned.1.call-done = bf16[512,1024]{1,0:T(8,128)(2,1)} async-done(((bf16[1024,1024]{1,0:T(8,128)(2,1)}), bf16[512,1024]{1,0:T(8,128)(2,1)}) %reduce-scatter.28.cloned.1.call-update) | async-done | bytes 1048592 | tf_op jit(solution)/shard_map/reduce_scatter | solution.py:49
  692.5 11.5 collective-permute-done.29
  704.7 25.6 %fusion.39 = (bf16[1024,2048]{1,0:T(8,128)(2,1)}, f32[1024,2048]{1,0:T(8,128)}) fusion(f32[2048]{0:T(1024)S(1)} %bitcast.435, bf16[1024,1024]{1,0:T(8,128)(2,1)} %all-gather.31.cloned.1.call-done, bf16[1024,2048]{1,0:T(8,128)(2,1)} %constant_dynamic-update-slice_fusion.8), kind=kOutput, calls=%fused_computation.83 | convolution fusion | flops 4433379328 | bytes 18882560 | tf_op jit(solution)/shard_map/dot_general | solution.py:178
  730.3 9.3 fusion.103
  739.9 27.6 %reduce-scatter.30.cloned.1.call-done = bf16[512,1024]{1,0:T(8,128)(2,1)} async-done(((bf16[1024,1024]{1,0:T(8,128)(2,1)}), bf16[512,1024]{1,0:T(8,128)(2,1)}) %reduce-scatter.30.cloned.1.call-update) | async-done | bytes 1048592 | tf_op jit(solution)/shard_map/reduce_scatter | solution.py:49
  776.4 32.7 %all-gather.33.cloned.1.call-done = bf16[1024,1024]{1,0:T(8,128)(2,1)} async-done(((bf16[512,1024]{1,0:T(8,128)(2,1)}), bf16[1024,1024]{1,0:T(8,128)(2,1)}) %all-gather.33.cloned.1.call-update) | async-done | bytes 2097168 | tf_op jit(solution)/shard_map/all_gather | solution.py:45
  809.0 12.5 convert_reduce_fusion
  821.5 40.1 %all-gather.53.cloned.1.call-done = bf16[1,1024,2048]{2,1,0:T(8,128)(2,1)} async-done(((bf16[1,64,2048]{2,1,0:T(8,128)(2,1)}), bf16[1,1024,2048]{2,1,0:T(8,128)(2,1)}) %all-gather.53.cloned.1.call-update) | async-done | bytes 4194320 | tf_op jit(solution)/shard_map/all_gather | solution.py:222
  861.6 9.3 fusion.106
  871.0 30.4 %reduce-scatter.32.cloned.1.call-done = bf16[512,1024]{1,0:T(8,128)(2,1)} async-done(((bf16[1024,1024]{1,0:T(8,128)(2,1)}), bf16[512,1024]{1,0:T(8,128)(2,1)}) %reduce-scatter.32.cloned.1.call-update) | async-done | bytes 1048592 | tf_op jit(solution)/shard_map/reduce_scatter | solution.py:49
  909.1 32.8 %all-gather.35.cloned.1.call-done = bf16[1024,1024]{1,0:T(8,128)(2,1)} async-done(((bf16[512,1024]{1,0:T(8,128)(2,1)}), bf16[1024,1024]{1,0:T(8,128)(2,1)}) %all-gather.35.cloned.1.call-update) | async-done | bytes 2097168 | tf_op jit(solution)/shard_map/all_gather | solution.py:45
  947.6 43.5 %while.46 = (s32[]{:T(128)}, bf16[2,512,3,512]{1,3,2,0:T(8,128)(2,1)}, bf16[2,512,512]{1,2,0:T(8,128)(2,1)}, s32[2,512]{1,0:T(2,128)S(1)}, bf16[2,512,512]{1,2,0...) while((s32[]{:T(128)}, ...), condition=%wide.region_27.28_spmd, body=%wide.region_25.27_spmd.sunk | while | flops 1379921920 | bytes 107076288 | solution.py:251
  995.8 7.7 bitcast_convert_fusion.1
  1003.8 31.8 %reduce-scatter.34.cloned.1.call-done = bf16[512,1024]{1,0:T(8,128)(2,1)} async-done(((bf16[1024,1024]{1,0:T(8,128)(2,1)}), bf16[512,1024]{1,0:T(8,128)(2,1)}) %reduce-scatter.34.cloned.1.call-update) | async-done | bytes 1048592 | tf_op jit(solution)/shard_map/reduce_scatter | solution.py:49
  1043.6 32.5 %all-gather.37.cloned.1.call-done = bf16[1024,1024]{1,0:T(8,128)(2,1)} async-done(((bf16[512,1024]{1,0:T(8,128)(2,1)}), bf16[1024,1024]{1,0:T(8,128)(2,1)}) %all-gather.37.cloned.1.call-update) | async-done | bytes 2097168 | tf_op jit(solution)/shard_map/all_gather | solution.py:45
  1076.1 11.9 convert_reduce_fusion.1
  1088.0 41.5 %all-gather.55.cloned.1.call-done = bf16[1,1024,2048]{2,1,0:T(8,128)(2,1)} async-done(((bf16[1,64,2048]{2,1,0:T(8,128)(2,1)}), bf16[1,1024,2048]{2,1,0:T(8,128)(2,1)}) %all-gather.55.cloned.1.call-update) | async-done | bytes 4194320 | tf_op jit(solution)/shard_map/all_gather | solution.py:222
  1129.6 9.4 fusion.109
  1139.1 30.4 %reduce-scatter.36.cloned.1.call-done = bf16[512,1024]{1,0:T(8,128)(2,1)} async-done(((bf16[1024,1024]{1,0:T(8,128)(2,1)}), bf16[512,1024]{1,0:T(8,128)(2,1)}) %reduce-scatter.36.cloned.1.call-update) | async-done | bytes 1048592 | tf_op jit(solution)/shard_map/reduce_scatter | solution.py:49
  1182.8 10.1 convolution_convert_fusion
  1194.4 8.3 convolution_convert_fusion.1
  1204.3 8.3 convolution_convert_fusion.2
  1215.4 8.3 convolution_convert_fusion.3
  1230.8 43.6 %while.47 = (s32[]{:T(128)}, bf16[2,512,3,512]{1,3,2,0:T(8,128)(2,1)}, bf16[2,512,512]{1,2,0:T(8,128)(2,1)}, s32[2,512]{1,0:T(2,128)S(1)}, bf16[2,512,512]{1,2,0...) while((s32[]{:T(128)}, ...), condition=%wide.region_36.37_spmd, body=%wide.region_34.36_spmd.sunk | while | flops 1379921920 | bytes 107076288 | solution.py:251
  1325.3 25.3 %reduce-scatter.56.cloned.1.call-done = f32[128,2]{1,0:T(8,128)} async-done(((f32[4096,2]{1,0:T(8,128)}), f32[128,2]{1,0:T(8,128)}) %reduce-scatter.56.cloned.1.call-update) | async-done | bytes 1040
  1352.1 131.6 %reduce-scatter.52.cloned.1.call-done = f32[32,4]{1,0:T(8,128)} async-done(((f32[1024,4]{1,0:T(8,128)}), f32[32,4]{1,0:T(8,128)}) %reduce-scatter.52.cloned.1.call-update) | async-done | bytes 528
  1485.2 71.4 %reduce-scatter.50.cloned.1.call-done = bf16[2048,64]{0,1:T(8,128)(2,1)} async-done(((bf16[2048,1024]{0,1:T(8,128)(2,1)}), bf16[2048,64]{0,1:T(8,128)(2,1)}) %reduce-scatter.50.cloned.1.call-update) | async-done | bytes 262160 | tf_op jit(solution)/shard_map/reduce_scatter | solution.py:307
  1556.5 75.5 %reduce-scatter.48.cloned.1.call-done = bf16[2048,64]{0,1:T(8,128)(2,1)} async-done(((bf16[2048,1024]{0,1:T(8,128)(2,1)}), bf16[2048,64]{0,1:T(8,128)(2,1)}) %reduce-scatter.48.cloned.1.call-update) | async-done | bytes 262160 | tf_op jit(solution)/shard_map/reduce_scatter | solution.py:307
  1634.0 73.8 %reduce-scatter.46.cloned.1.call-done = bf16[64,2048]{1,0:T(8,128)(2,1)} async-done(((bf16[1024,2048]{1,0:T(8,128)(2,1)}), bf16[64,2048]{1,0:T(8,128)(2,1)}) %reduce-scatter.46.cloned.1.call-update) | async-done | bytes 262160 | tf_op jit(solution)/shard_map/reduce_scatter | solution.py:304
  1707.8 75.3 %reduce-scatter.44.cloned.1.call-done = bf16[64,2048]{1,0:T(8,128)(2,1)} async-done(((bf16[1024,2048]{1,0:T(8,128)(2,1)}), bf16[64,2048]{1,0:T(8,128)(2,1)}) %reduce-scatter.44.cloned.1.call-update) | async-done | bytes 262160 | tf_op jit(solution)/shard_map/reduce_scatter | solution.py:304
  1785.2 133.0 %reduce-scatter.54.cloned.1.call-done = f32[32,12]{1,0:T(8,128)} async-done(((f32[1024,12]{1,0:T(8,128)}), f32[32,12]{1,0:T(8,128)}) %reduce-scatter.54.cloned.1.call-update) | async-done | bytes 1552
  1919.6 55.4 %reduce-scatter.42.cloned.1.call-done = bf16[512,64]{0,1:T(8,128)(2,1)} async-done(((bf16[512,1024]{0,1:T(8,128)(2,1)}), bf16[512,64]{0,1:T(8,128)(2,1)}) %reduce-scatter.42.cloned.1.call-update) | async-done | bytes 65552 | tf_op jit(solution)/shard_map/reduce_scatter | solution.py:301
  1975.1 60.5 %reduce-scatter.40.cloned.1.call-done = bf16[512,64]{0,1:T(8,128)(2,1)} async-done(((bf16[512,1024]{0,1:T(8,128)(2,1)}), bf16[512,64]{0,1:T(8,128)(2,1)}) %reduce-scatter.40.cloned.1.call-update) | async-done | bytes 65552 | tf_op jit(solution)/shard_map/reduce_scatter | solution.py:301
  2037.2 171.4 %all-reduce.5.cloned.1.call-done = (bf16[3,1024,512]{2,0,1:T(4,128)(2,1)}, bf16[3,1024,512]{2,0,1:T(4,128)(2,1)}) async-done(((bf16[3,1024,512]{2,0,1:T(4,128)(2,1)}, bf16[3,1024,512]{2,0,1:T(4,128)(2,1)}), (bf16[3,1024,512]{2,0,1:T(4,128)(2,1)}, bf16[3,1024,512]{2,0,1:T(4,128)(2,1)})) %all-reduce.5.cloned.1.call-update) | async-done | bytes 6291472
  2212.1 31.1 %reduce-scatter.38.cloned.1.call-done = bf16[512,1024]{1,0:T(8,128)(2,1)} async-done(((bf16[1024,1024]{1,0:T(8,128)(2,1)}), bf16[512,1024]{1,0:T(8,128)(2,1)}) %reduce-scatter.38.cloned.1.call-update) | async-done | bytes 1048592 | tf_op jit(solution)/shard_map/reduce_scatter | solution.py:49
  (589 shorter events, 448.4 us)
Async XLA Ops:
  7.2 116.7 %all-gather.25.cloned.1.call-start = ((), (), s32[]{:S(2)}) async-start(), calls=%async_computation.17 | async-start | bytes 3145728 | tf_op jit(solution)/shard_map/all_gather | solution.py:45
  7.9 116.0 %all-gather.41.cloned.1.call-start = ((), (), s32[]{:S(2)}) async-start(), calls=%async_computation.39 | async-start | bytes 3342336 | tf_op jit(solution)/shard_map/all_gather | solution.py:154
  9.9 142.2 %all-gather.43.cloned.1.call-start = ((), (), s32[]{:S(2)}) async-start(), calls=%async_computation.40 | async-start | bytes 1114112 | tf_op jit(solution)/shard_map/all_gather | solution.py:155
  11.6 242.8 %reduce-scatter.24.cloned.1.call-start = ((), (), s32[]{:S(2)}) async-start(), calls=%async_computation.18 | async-start | bytes 3145728 | tf_op jit(solution)/shard_map/reduce_scatter | solution.py:49
  156.3 244.2 %all-gather.27.cloned.1.call-start = ((), (), s32[]{:S(2)}) async-start(), calls=%async_computation.19 | async-start | bytes 3145728 | tf_op jit(solution)/shard_map/all_gather | solution.py:45
  259.6 166.7 %all-gather.45.cloned.1.call-start = ((), (), s32[]{:S(2)}) async-start(), calls=%async_computation.41 | async-start | bytes 4456448 | tf_op jit(solution)/shard_map/all_gather | solution.py:157
  262.0 76.5 %collective-permute-start = (bf16[64,2048]{1,0:T(8,128)(2,1)S(1)}, bf16[64,2048]{1,0:T(8,128)(2,1)S(1)}, u32[]{:S(2)}, u32[]{:S(2)}) collective-permute-start(bf16[64,2048]{1,0:T(8,128)(2,1)S(1)} %get-tuple-element.416), channel_id=1, source_target_pairs={{0,2},{2,4},{4,6},{6,8},{8,10},{10,12},{12,14},{14,16},{16,18},{18... | collective-permute-start | bytes 786440 | tf_op jit(solution)/shard_map/ppermute | solution.py:21
  262.0 76.5 %collective-permute-start.1 = (bf16[64,2048]{1,0:T(8,128)(2,1)S(1)}, bf16[64,2048]{1,0:T(8,128)(2,1)S(1)}, u32[]{:S(2)}, u32[]{:S(2)}) collective-permute-start(bf16[64,2048]{1,0:T(8,128)(2,1)S(1)} %get-tuple-element.416), channel_id=1, source_target_pairs={{0,30},{2,0},{4,2},{6,4},{8,6},{10,8},{12,10},{14,12},{16,14},{18,... | collective-permute-start | bytes 786440 | tf_op jit(solution)/shard_map/ppermute | solution.py:24
  268.7 194.8 %reduce-scatter.26.cloned.1.call-start = ((), (), s32[]{:S(2)}) async-start(), calls=%async_computation.20 | async-start | bytes 3145728 | tf_op jit(solution)/shard_map/reduce_scatter | solution.py:49
  338.6 9.9 collective-permute-start.2
  338.6 9.9 collective-permute-start.3
  382.9 9.2 collective-permute-start.13
  435.7 75.3 %all-gather.47.cloned.1.call-start = ((), (), s32[]{:S(2)}) async-start(), calls=%async_computation.42 | async-start | bytes 3342336 | tf_op jit(solution)/shard_map/all_gather | solution.py:154
  436.4 108.6 %all-gather.29.cloned.1.call-start = ((), (), s32[]{:S(2)}) async-start(), calls=%async_computation.21 | async-start | bytes 3145728 | tf_op jit(solution)/shard_map/all_gather | solution.py:45
  468.5 116.6 %all-gather.49.cloned.1.call-start = ((), (), s32[]{:S(2)}) async-start(), calls=%async_computation.43 | async-start | bytes 1114112 | tf_op jit(solution)/shard_map/all_gather | solution.py:155
  469.1 150.8 %reduce-scatter.28.cloned.1.call-start = ((), (), s32[]{:S(2)}) async-start(), calls=%async_computation.22 | async-start | bytes 3145728 | tf_op jit(solution)/shard_map/reduce_scatter | solution.py:49
  589.0 115.8 %all-gather.31.cloned.1.call-start = ((), (), s32[]{:S(2)}) async-start(), calls=%async_computation.23 | async-start | bytes 3145728 | tf_op jit(solution)/shard_map/all_gather | solution.py:45
  624.9 105.4 %all-gather.51.cloned.1.call-start = ((), (), s32[]{:S(2)}) async-start(), calls=%async_computation.44 | async-start | bytes 4456448 | tf_op jit(solution)/shard_map/all_gather | solution.py:157
  625.0 8.7 collective-permute-start.15
  625.0 9.3 collective-permute-start.16
  629.5 138.0 %reduce-scatter.30.cloned.1.call-start = ((), (), s32[]{:S(2)}) async-start(), calls=%async_computation.24 | async-start | bytes 3145728 | tf_op jit(solution)/shard_map/reduce_scatter | solution.py:49
  642.9 8.8 collective-permute-start.20
  650.8 8.8 collective-permute-start.21
  660.4 8.6 collective-permute-start.24
  668.2 13.6 collective-permute-start.25
  669.0 13.6 collective-permute-start.26
  682.5 9.3 collective-permute-start.28
  690.3 13.7 collective-permute-start.29
  739.6 69.4 %all-gather.33.cloned.1.call-start = ((), (), s32[]{:S(2)}) async-start(), calls=%async_computation.25 | async-start | bytes 3145728 | tf_op jit(solution)/shard_map/all_gather | solution.py:45
  775.7 85.9 %all-gather.53.cloned.1.call-start = ((), (), s32[]{:S(2)}) async-start(), calls=%async_computation.45 | async-start | bytes 4456448 | tf_op jit(solution)/shard_map/all_gather | solution.py:222
  776.3 125.1 %reduce-scatter.32.cloned.1.call-start = ((), (), s32[]{:S(2)}) async-start(), calls=%async_computation.26 | async-start | bytes 3145728 | tf_op jit(solution)/shard_map/reduce_scatter | solution.py:49
  871.0 70.9 %all-gather.35.cloned.1.call-start = ((), (), s32[]{:S(2)}) async-start(), calls=%async_computation.27 | async-start | bytes 3145728 | tf_op jit(solution)/shard_map/all_gather | solution.py:45
  908.6 127.0 %reduce-scatter.34.cloned.1.call-start = ((), (), s32[]{:S(2)}) async-start(), calls=%async_computation.28 | async-start | bytes 3145728 | tf_op jit(solution)/shard_map/reduce_scatter | solution.py:49
  1003.6 72.5 %all-gather.37.cloned.1.call-start = ((), (), s32[]{:S(2)}) async-start(), calls=%async_computation.29 | async-start | bytes 3145728 | tf_op jit(solution)/shard_map/all_gather | solution.py:45
  1042.8 86.8 %all-gather.55.cloned.1.call-start = ((), (), s32[]{:S(2)}) async-start(), calls=%async_computation.46 | async-start | bytes 4456448 | tf_op jit(solution)/shard_map/all_gather | solution.py:222
  1043.5 126.0 %reduce-scatter.36.cloned.1.call-start = ((), (), s32[]{:S(2)}) async-start(), calls=%async_computation.30 | async-start | bytes 3145728 | tf_op jit(solution)/shard_map/reduce_scatter | solution.py:49
  1139.1 84.9 %all-gather.39.cloned.1.call-start = ((), (), s32[]{:S(2)}) async-start(), calls=%async_computation.31 | async-start | bytes 3145728 | tf_op jit(solution)/shard_map/all_gather | solution.py:45
  1178.0 172.6 %reduce-scatter.56.cloned.1.call-start = ((), (), s32[]{:S(2)}) async-start(), calls=%async_computation.49 | async-start | bytes 2162688
  1180.6 303.1 %reduce-scatter.52.cloned.1.call-start = ((), (), s32[]{:S(2)}) async-start(), calls=%async_computation.47 | async-start | bytes 540672
  1182.7 373.8 %reduce-scatter.50.cloned.1.call-start = ((), (), s32[]{:S(2)}) async-start(), calls=%async_computation.38 | async-start | bytes 4456448 | tf_op jit(solution)/shard_map/reduce_scatter | solution.py:307
  1192.8 439.1 %reduce-scatter.48.cloned.1.call-start = ((), (), s32[]{:S(2)}) async-start(), calls=%async_computation.37 | async-start | bytes 4456448 | tf_op jit(solution)/shard_map/reduce_scatter | solution.py:307
  1202.7 505.1 %reduce-scatter.46.cloned.1.call-start = ((), (), s32[]{:S(2)}) async-start(), calls=%async_computation.36 | async-start | bytes 4456448 | tf_op jit(solution)/shard_map/reduce_scatter | solution.py:304
  1212.7 570.4 %reduce-scatter.44.cloned.1.call-start = ((), (), s32[]{:S(2)}) async-start(), calls=%async_computation.35 | async-start | bytes 4456448 | tf_op jit(solution)/shard_map/reduce_scatter | solution.py:304
  1223.7 694.5 %reduce-scatter.54.cloned.1.call-start = ((), (), s32[]{:S(2)}) async-start(), calls=%async_computation.48 | async-start | bytes 540672
  1279.0 696.0 %reduce-scatter.42.cloned.1.call-start = ((), (), s32[]{:S(2)}) async-start(), calls=%async_computation.34 | async-start | bytes 1114112 | tf_op jit(solution)/shard_map/reduce_scatter | solution.py:301
  1283.0 752.5 %reduce-scatter.40.cloned.1.call-start = ((), (), s32[]{:S(2)}) async-start(), calls=%async_computation.33 | async-start | bytes 1114112 | tf_op jit(solution)/shard_map/reduce_scatter | solution.py:301
  1287.2 921.3 %all-reduce.5.cloned.1.call-start = ((), (), s32[]{:S(2)}) async-start(), calls=%async_computation.50 | async-start | bytes 16777216
  1315.6 927.6 %reduce-scatter.38.cloned.1.call-start = ((), (), s32[]{:S(2)}) async-start(), calls=%async_computation.32 | async-start | bytes 3145728 | tf_op jit(solution)/shard_map/reduce_scatter | solution.py:49
  (113 other events, 5385.9 us)
Sparse Core Ops, SparseCore 0:
  9.6 44.2 all-gather.24
  56.6 47.2 all-gather.40
  106.6 36.7 all-gather.42
  156.5 37.5 reduce-scatter.23
  259.8 31.2 all-gather.26
  293.9 59.0 all-gather.44
  435.8 27.7 reduce-scatter.25
  465.7 45.2 all-gather.46
  513.1 31.9 all-gather.28
  547.1 37.9 all-gather.48
  589.1 30.7 reduce-scatter.27
  625.0 33.0 all-gather.30
  660.6 53.7 all-gather.50
  739.7 27.6 reduce-scatter.29
  775.8 33.1 all-gather.32
  811.0 50.5 all-gather.52
  871.1 30.3 reduce-scatter.31
  908.7 33.0 all-gather.34
  1003.7 31.8 reduce-scatter.33
  1042.9 33.1 all-gather.36
  1078.8 50.7 all-gather.54
  1139.2 30.3 reduce-scatter.35
  1178.1 33.1 all-gather.38
  1213.5 137.0 reduce-scatter.55
  1353.4 130.2 reduce-scatter.51
  1487.9 68.5 reduce-scatter.49
  1560.2 71.7 reduce-scatter.47
  1636.3 71.4 reduce-scatter.45
  1711.7 71.3 reduce-scatter.43
  1785.3 132.8 reduce-scatter.53
  1921.8 53.2 reduce-scatter.41
  1979.1 56.3 reduce-scatter.39
  2039.2 169.2 all-reduce.4
  2211.4 31.6 reduce-scatter.37
